TPU v7x, 256 devices: a whole 4x4x8 slice. The times are simulated.
256 devices in a mesh: prow: 16 (over z, core), pcol: 16 (over y, x).
Axes of the slice: x: 4, y: 4, z: 8, core: 2. Of those that a mesh axis runs over, the one named last changes fastest.
Arguments:
- diag_tile: float32 [512, 512], P('prow', 'pcol'), as said below
- panel: float32 [2, 16, 512, 512], P(None, 'prow', None, 'pcol'), may hold values from -0.3 to 0.3
- trailing: float32 [2, 16, 512, 2, 16, 512], P(None, 'prow', None, None, 'pcol'), may hold values from -6 to 6
- kept: int32 [33, 33], replicated, may hold values from 0 to 1, as said below
- precision: int32 [33, 33], replicated, may hold values from 0 to 1, as said below
- tile_scale: float32 [33, 33], replicated, may hold values from 0.5 to 4
Outputs:
- diag_factor: float32 [512, 512], P('prow', 'pcol')
- factor: float32 [2, 16, 512, 512], P(None, 'prow', None, 'pcol')
- updated: float32 [2, 16, 512, 2, 16, 512], P(None, 'prow', None, None, 'pcol')
Inputs may be any that keep to these rules, and one draw needn't show every extreme that they name: kept is symmetric, 1 on the diagonal, and has zeros in every draw; tiles are kept by a distance between the tiles' places. precision is symmetric, 1 on the diagonal, has zeros in every draw, and is 1 only where kept is 1. diag_tile is symmetric positive definite with smallest eigenvalue at least 0.1.
All inputs are finite; a program needn't handle non-finite values.
Results may differ from a plain program's by a relative error of at most 0.0003.
The roundings to bfloat16 on the way count: a program that leaves them out, or rounds other values in their place, can miss the bound.
Values sent between devices are 32-bit elements; how exact they have to be, the bound alone decides.
A program may use at most 64 MiB of HBM per device.

v0:
```python
import jax
import jax.numpy as jnp
from jax import lax
from jax.experimental import pallas as pl
from jax.experimental.pallas import tpu as pltpu
from jax.sharding import PartitionSpec as P

BLOCK = 128
PANEL = 16
SUB = 8
FULL = lax.Precision.HIGHEST


def dot_f32(a, b, ca, cb):
    return lax.dot_general(
        a, b, (((ca,), (cb,)), ((), ())), precision=FULL, preferred_element_type=jnp.float32
    )


def factor_block(work):
    sub = lax.broadcasted_iota(jnp.int32, (SUB, BLOCK), 0)
    halves = PANEL // SUB
    for base in range(0, BLOCK, PANEL):
        rows = [work[base + SUB * h : base + SUB * (h + 1), :] for h in range(halves)]
        left = [r[:, :BLOCK] for r in rows]
        right = [r[:, BLOCK:] for r in rows]
        cols = {}
        for k in range(PANEL):
            for h in range(k // SUB, halves):
                cols[k, h] = jnp.broadcast_to(
                    left[h][:, base + k : base + k + 1], (SUB, BLOCK)
                )
        scale = [jnp.ones((SUB, BLOCK), jnp.float32) for _ in range(halves)]
        for m in range(PANEL):
            own, at = m // SUB, m % SUB
            pivot = jnp.broadcast_to(cols[m, own][at : at + 1, :], (SUB, BLOCK))
            root = lax.rsqrt(pivot)
            scale[own] = jnp.where(sub == at, root, scale[own])
            lower = {h: cols[m, h] * root for h in range(own, halves)}
            for k in range(m + 1, PANEL):
                factor = jnp.broadcast_to(
                    lower[k // SUB][k % SUB : k % SUB + 1, :], (SUB, BLOCK)
                )
                for h in range(k // SUB, halves):
                    cols[k, h] = cols[k, h] - lower[h] * factor
            source_left = jnp.broadcast_to(left[own][at : at + 1, :], (SUB, BLOCK)) * root
            source_right = jnp.broadcast_to(right[own][at : at + 1, :], (SUB, BLOCK)) * root
            for h in range(own, halves):
                weight = jnp.where(sub > at, lower[h], 0.0) if h == own else lower[h]
                left[h] = left[h] - weight * source_left
                right[h] = right[h] - weight * source_right
        left = [x * s for x, s in zip(left, scale)]
        right = [x * s for x, s in zip(right, scale)]
        upper = jnp.concatenate(left, 0)
        both = jnp.concatenate([upper, jnp.concatenate(right, 0)], 1)
        work[base : base + PANEL, :] = both
        rest = base + PANEL
        if rest < BLOCK:
            change = dot_f32(upper.T[rest:, :], both, 1, 0)
            work[rest:, :] = work[rest:, :] - change


def cholesky_kernel(gathered, u_ref, v_ref, trail, extra, work):
    width = u_ref.shape[0]
    assemble(gathered, trail, extra)
    u_ref[...] = jnp.zeros_like(u_ref)
    v_ref[...] = jnp.zeros_like(v_ref)
    extra[...] = jnp.zeros_like(extra)
    row = lax.broadcasted_iota(jnp.int32, (BLOCK, BLOCK), 0)
    col = lax.broadcasted_iota(jnp.int32, (BLOCK, BLOCK), 1)
    eye = (row == col).astype(jnp.float32)
    for base in range(0, width, BLOCK):
        here = slice(base, base + BLOCK)
        end = base + BLOCK
        work[:, :BLOCK] = trail[here, here]
        work[:, BLOCK:] = eye
        factor_block(work)
        inverse = work[:, BLOCK:]
        u_ref[here, here] = jnp.where(row <= col, work[:, :BLOCK], 0.0)
        v_ref[here, here] = inverse
        if base:
            v_ref[here, :base] = dot_f32(inverse, extra[here, :base], 1, 0)
        if end < width:
            upper = dot_f32(inverse, trail[here, end:], 1, 0)
            u_ref[here, end:] = upper
            turned = upper.T
            for low in range(end, width, BLOCK):
                piece = turned[low - end : low - end + BLOCK, :]
                trail[low : low + BLOCK, low:] = trail[low : low + BLOCK, low:] - dot_f32(
                    piece, upper[:, low - end :], 1, 0
                )
            extra[end:, :end] = extra[end:, :end] - dot_f32(turned, v_ref[here, :end], 1, 0)


def factorize(a, width):
    shape = jax.ShapeDtypeStruct((width, width), jnp.float32)
    vmem = pl.BlockSpec(memory_space=pltpu.VMEM)
    return pl.pallas_call(
        cholesky_kernel,
        out_shape=(shape, shape),
        in_specs=[vmem],
        out_specs=(vmem, vmem),
        scratch_shapes=[
            pltpu.VMEM((width, width), jnp.float32),
            pltpu.VMEM((width, width), jnp.float32),
            pltpu.VMEM((BLOCK, 2 * BLOCK), jnp.float32),
        ],
        compiler_params=pltpu.CompilerParams(vmem_limit_bytes=32 << 20),
        cost_estimate=pl.CostEstimate(flops=1 << 32, bytes_accessed=4 << 20, transcendentals=0),
        name="factorize",
    )(a)


def split(x):
    high = x.astype(jnp.bfloat16)
    return high, (x - high.astype(jnp.float32)).astype(jnp.bfloat16)


def assemble(gathered, a_ref, direct):
    count, width = gathered.shape[0], a_ref.shape[0]
    side = width // count
    per = BLOCK // side
    lane = lax.broadcasted_iota(jnp.int32, (SUB, BLOCK), 1) // side
    for q in range(count):
        held = {}
        for o in range(count // 2 + 1):
            if o < count // 2 or q < count // 2:
                held[(q + o) % count] = gathered[q, o]
        for g in range(side // SUB):
            for tile in range(count // per):
                total = jnp.zeros((SUB, BLOCK), jnp.float32)
                for e in range(per):
                    piece = held.get(tile * per + e)
                    if piece is not None:
                        shift = (e - g) % per * side
                        moved = pltpu.roll(piece, shift, 1) if shift else piece
                        total = jnp.where(lane == e, moved, total)
                low = q * side + g * SUB
                direct[low : low + SUB, tile * BLOCK : (tile + 1) * BLOCK] = total
    row = lax.broadcasted_iota(jnp.int32, (BLOCK, BLOCK), 0) // side
    col = lax.broadcasted_iota(jnp.int32, (BLOCK, BLOCK), 1) // side
    for i in range(0, width, BLOCK):
        for j in range(i, width, BLOCK):
            here = direct[i : i + BLOCK, j : j + BLOCK]
            there = direct[j : j + BLOCK, i : i + BLOCK].T
            if i == j:
                there = jnp.where(row == col, 0.0, there)
            a_ref[i : i + BLOCK, j : j + BLOCK] = here + there


def update_kernel(
    kept, near, scale, u_ref, v_ref, rows_ref, cols_ref, trailing, out_hbm, factor_ref, diag_ref,
    current, result, srow, frow_h, frow_l, scol_h, scol_l, turned, sems,
):
    tiles, pieces, side, width = rows_ref.shape
    p, q = lax.axis_index("prow"), lax.axis_index("pcol")
    rows_all = lax.axis_size("prow")
    cols_all = lax.axis_size("pcol")
    half = current.shape[0] // tiles
    chunks = width // BLOCK
    loads = [
        pltpu.make_async_copy(
            trailing.at[pl.ds(r * half, half)], current.at[pl.ds(r * half, half)], sems.at[r]
        )
        for r in range(tiles)
    ]
    for load in loads:
        load.start()
    turned[...] = u_ref[pl.ds(pl.multiple_of(q * side, side), side), :].T
    diag_ref[...] = turned[pl.ds(pl.multiple_of(p * side, side), side), :]
    mid = width // 2

    def solve(piece):
        top = dot_f32(v_ref[:mid, :mid], piece[:mid, :], 1, 0)
        low = dot_f32(v_ref[mid:, :], piece, 1, 0)
        return jnp.concatenate([top, low], 0)

    for r in range(tiles):
        keep = kept[r * rows_all + p + 1, 0].astype(jnp.float32)
        solved = solve(rows_ref[r].reshape(width, width)) * keep
        srow[r] = solved
        high, low = split(solved.T)
        frow_h[r] = high
        frow_l[r] = low
    for t in range(tiles):
        keep = kept[t * cols_all + q + 1, 0].astype(jnp.float32)
        high, low = split(solve(cols_ref[t].reshape(width, width)) * keep)
        scol_h[t] = high
        scol_l[t] = low
    for r in range(tiles):
        factor_ref[r] = srow[r, pl.ds(pl.multiple_of(q * side, side), side), :]

    def dot_half(a, b):
        return jnp.dot(a, b, preferred_element_type=jnp.float32)

    stores = []
    for r in range(tiles):
        loads[r].wait()
        for t in range(tiles):
            i, j = r * rows_all + p + 1, t * cols_all + q + 1
            is_kept = kept[i, j] == 1
            is_near = near[i, j] == 1

            def place(l):
                return pl.ds(r * half + t * chunks + l, width, stride=tiles * chunks)

            @pl.when(jnp.logical_and(is_kept, is_near))
            def _():
                exact = dot_half(frow_h[r], scol_h[t]) + (
                    dot_half(frow_h[r], scol_l[t]) + dot_half(frow_l[r], scol_h[t])
                )
                for l in range(chunks):
                    result[place(l), :] = (
                        current[place(l), :] - exact[:, l * BLOCK : (l + 1) * BLOCK]
                    )

            @pl.when(jnp.logical_and(is_kept, jnp.logical_not(is_near)))
            def _():
                rough = dot_half(frow_h[r], scol_h[t]) / scale[i, j]
                for l in range(chunks):
                    far = current[place(l), :] - rough[:, l * BLOCK : (l + 1) * BLOCK]
                    result[place(l), :] = far.astype(jnp.bfloat16).astype(jnp.float32)

            @pl.when(jnp.logical_not(is_kept))
            def _():
                for l in range(chunks):
                    result[place(l), :] = jnp.zeros((width, BLOCK), jnp.float32)

        store = pltpu.make_async_copy(
            result.at[pl.ds(r * half, half)], out_hbm.at[pl.ds(r * half, half)], sems.at[tiles + r]
        )
        store.start()
        stores.append(store)
    for store in stores:
        store.wait()


def update(kept, near, scale, upper, inverse, rows, cols, trailing):
    tiles, pieces, side, width = rows.shape
    vmem = pl.BlockSpec(memory_space=pltpu.VMEM)
    smem = pl.BlockSpec(memory_space=pltpu.SMEM)
    hbm = pl.BlockSpec(memory_space=pl.ANY)
    flat = trailing.reshape(trailing.size // BLOCK, BLOCK)
    shape = jax.ShapeDtypeStruct
    return pl.pallas_call(
        update_kernel,
        out_shape=(
            shape(flat.shape, jnp.float32),
            shape((tiles, side, width), jnp.float32),
            shape((side, side), jnp.float32),
        ),
        in_specs=[smem, smem, smem, vmem, vmem, vmem, vmem, hbm],
        out_specs=(hbm, vmem, vmem),
        scratch_shapes=[
            pltpu.VMEM(flat.shape, jnp.float32),
            pltpu.VMEM(flat.shape, jnp.float32),
            pltpu.VMEM((tiles, width, width), jnp.float32),
            pltpu.VMEM((tiles, width, width), jnp.bfloat16),
            pltpu.VMEM((tiles, width, width), jnp.bfloat16),
            pltpu.VMEM((tiles, width, width), jnp.bfloat16),
            pltpu.VMEM((tiles, width, width), jnp.bfloat16),
            pltpu.VMEM((width, side), jnp.float32),
            pltpu.SemaphoreType.DMA((2 * tiles,)),
        ],
        compiler_params=pltpu.CompilerParams(vmem_limit_bytes=56 << 20),
        name="update",
    )(kept, near, scale, upper, inverse, rows, cols, flat)


def exchange_kernel(
    pack, own, gathered, rows, cols, first, turned,
    local_sems, turn_sems, send1, recv1, send2, recv2, send3, recv3, send4, recv4,
):
    p, q = lax.axis_index("prow"), lax.axis_index("pcol")
    n, m = lax.axis_size("prow"), lax.axis_size("pcol")
    keep = gathered.shape[1]
    mesh_id = pl.DeviceIdType.MESH

    def others(me, count, body):
        def step(s, carry):
            body(lax.rem(me + s, count))
            return carry

        lax.fori_loop(1, count, step, 0)

    barrier = pltpu.get_barrier_semaphore()

    def greet(a, b):
        pl.semaphore_signal(barrier, inc=1, device_id=(a, b), device_id_type=mesh_id)

    others(p, n, lambda a: greet(a, q))
    others(q, m, lambda b: greet(p, b))

    @pl.when(p != q)
    def _():
        greet(q, p)

    pl.semaphore_wait(barrier, n + m - 2 + (p != q).astype(jnp.int32))

    def remote(src, dst, send, recv, a, b):
        return pltpu.make_async_remote_copy(
            src_ref=src, dst_ref=dst, send_sem=send, recv_sem=recv,
            device_id=(a, b), device_id_type=mesh_id,
        )

    slot = lax.rem(p + m - q, m)
    mine = pltpu.make_async_copy(pack, first.at[slot], local_sems.at[0])
    mine.start()

    def first_copy(a, sender):
        at = lax.rem(sender + m - q, m)
        return remote(pack, first.at[at], send1.at[a], recv1.at[sender], a, q)

    others(p, n, lambda a: first_copy(a, p).start())

    swap = remote(own, turned, turn_sems.at[0], turn_sems.at[1], q, p)
    stay = pltpu.make_async_copy(own, turned, local_sems.at[1])

    @pl.when(p != q)
    def _():
        swap.start()

    @pl.when(p == q)
    def _():
        stay.start()

    mine.wait()
    others(p, n, lambda a: first_copy(a, a).wait_recv())

    part = first.at[pl.ds(0, keep)]
    block = pltpu.make_async_copy(part, gathered.at[q], local_sems.at[2])
    block.start()

    def second_copy(b, sender):
        return remote(part, gathered.at[sender], send2.at[b], recv2.at[sender], p, b)

    others(q, m, lambda b: second_copy(b, q).start())

    @pl.when(p != q)
    def _():
        swap.wait()

    @pl.when(p == q)
    def _():
        stay.wait()

    core = lax.rem(p, 2)
    other = p + 1 - 2 * core
    held = pltpu.make_async_copy(turned.at[core], cols.at[core, p], local_sems.at[3])
    held.start()

    def fourth_copy(a, sender, tile):
        return remote(
            turned.at[tile], cols.at[tile, sender], send4.at[a], recv4.at[sender], a, q
        )

    others(p, n, lambda a: fourth_copy(a, p, lax.rem(a, 2)).start())

    block.wait()
    others(q, m, lambda b: second_copy(b, b).wait_recv())

    whole = pltpu.make_async_copy(own, rows.at[:, q], local_sems.at[4])
    whole.start()

    def third_copy(b, sender):
        return remote(own, rows.at[:, sender], send3.at[b], recv3.at[sender], p, b)

    others(q, m, lambda b: third_copy(b, q).start())

    held.wait()
    others(p, n, lambda a: fourth_copy(a, a, core).wait_recv())
    partner = remote(cols.at[core], cols.at[core], turn_sems.at[2], turn_sems.at[3], other, q)
    partner.start()
    whole.wait()
    others(q, m, lambda b: third_copy(b, b).wait_recv())
    partner.wait()
    others(p, n, lambda a: first_copy(a, p).wait_send())
    others(q, m, lambda b: second_copy(b, q).wait_send())
    others(q, m, lambda b: third_copy(b, q).wait_send())
    others(p, n, lambda a: fourth_copy(a, p, lax.rem(a, 2)).wait_send())


def exchange(pack, own):
    n, m = lax.axis_size("prow"), lax.axis_size("pcol")
    tiles, side, width = own.shape
    vmem = pl.BlockSpec(memory_space=pltpu.VMEM)
    shape = jax.ShapeDtypeStruct
    dma = pltpu.SemaphoreType.DMA
    return pl.pallas_call(
        exchange_kernel,
        out_shape=(
            shape((m, n // 2 + 1, SUB, BLOCK), jnp.float32),
            shape((tiles, m, side, width), jnp.float32),
            shape((tiles, n, side, width), jnp.float32),
        ),
        in_specs=[vmem, vmem],
        out_specs=(vmem, vmem, vmem),
        scratch_shapes=[
            pltpu.VMEM((n, SUB, BLOCK), jnp.float32),
            pltpu.VMEM((tiles, side, width), jnp.float32),
            dma((5,)), dma((4,)),
            dma((n,)), dma((n,)), dma((m,)), dma((m,)),
            dma((m,)), dma((m,)), dma((n,)), dma((n,)),
        ],
        compiler_params=pltpu.CompilerParams(
            collective_id=0, has_side_effects=True, vmem_limit_bytes=32 << 20
        ),
        name="exchange",
    )(pack, own)


def per_device(diag_tile, panel, trailing, kept, precision, tile_scale):
    side = diag_tile.shape[0]
    own = jnp.transpose(panel[:, 0], (0, 2, 1))
    pack = diag_tile.T.reshape(side // SUB, SUB, side).transpose(1, 0, 2).reshape(SUB, BLOCK)
    gathered, rows, cols = exchange(pack, own)
    upper, inverse = factorize(gathered, panel.shape[2])
    updated, factor, diag_out = update(
        kept, precision, tile_scale, upper, inverse, rows, cols, trailing
    )
    factor_out = jnp.transpose(factor, (0, 2, 1))[:, None]
    return (diag_out, factor_out, updated.reshape(trailing.shape))


def solution(mesh):
    in_specs = (
        P("prow", "pcol"),
        P(None, "prow", None, "pcol"),
        P(None, "prow", None, None, "pcol", None),
        P(),
        P(),
        P(),
    )
    out_specs = (
        P("prow", "pcol"),
        P(None, "prow", None, "pcol"),
        P(None, "prow", None, None, "pcol", None),
    )
    return jax.shard_map(
        per_device, mesh=mesh, in_specs=in_specs, out_specs=out_specs, check_vma=False
    )
```

profile of v0, /device:TPU:176, one launch (start us, length us, event | category | flops | bytes accessed | tf_op | source)
XLA Modules:
  0.0 105.3 jit_solution(8090967028151520874)
XLA Ops:
  0.6 0.8 copy.12
  1.4 0.1 reshape.19.pack
  1.5 0.0 copy-start.4
  1.5 0.9 copy-done.4
  2.4 66.8 %exchange.1 = (f32[16,9,8,128]{3,2,1,0:T(8,128)S(1)}, f32[2,16,32,512]{3,2,1,0:T(8,128)S(1)}, f32[2,16,32,512]{3,2,1,0:T(8,128)S(1)}) custom-call(f32[8,128]{1,0:T(8,128)S(1)} %reshape.19.pack, f32[2,32,512]{2,1,0:T(8,128)S(1)} %bitcast.15), custom_call_target="tpu_custom_call" | custom-call | tf_op jit(solution)/shard_map/exchange/pallas_call | solution.py:389
  69.2 0.0 copy-start
  69.2 1.3 %copy-done = f32[2,16,32,512]{3,2,1,0:T(8,128)} copy-done((f32[2,16,32,512]{3,2,1,0:T(8,128)}, f32[2,16,32,512]{3,2,1,0:T(8,128)S(1)}, u32[]{:S(2)}) %copy-start) | copy-done | bytes 2097176
  70.6 0.0 copy-start.1
  70.6 19.3 %factorize.1 = (f32[512,512]{1,0:T(8,128)S(1)}, f32[512,512]{1,0:T(8,128)S(1)}) custom-call(f32[16,9,8,128]{3,2,1,0:T(8,128)S(1)} %get-tuple-element.11.gathered), custom_call_target="tpu_custom_call" | custom-call | flops 4294967296 | bytes 4194304 | tf_op jit(solution)/shard_map/factorize/pallas_call | solution.py:98
  89.9 0.0 copy-done.1
  89.9 0.0 copy-start.2
  89.9 1.0 copy-done.2
  90.9 0.0 copy-start.3
  90.9 1.0 copy-done.3
  91.9 13.3 %update.1 = (f32[8192,128]{1,0:T(8,128)}, f32[2,32,512]{2,1,0:T(8,128)}, f32[32,32]{1,0:T(8,128)}) custom-call(s32[33,33]{1,0:T(8,128)} %kept.1, s32[33,33]{1,0:T(8,128)} %near.1, f32[33,33]{1,0:T(8,128)} %scale.1, f32[512,512]{1,0:T(8,128)} %copy-done.2, f32[512,512]{1,0:T(8,128)} %copy-done.3, f32[2,16,32,512]{3,2,1,0:T(8,128)} %copy-done, ...), custom_call_target="tpu_custom_call" | custom-call | tf_op jit(solution)/shard_map/update/pallas_call | solution.py:245
  (1 shorter events, 0.0 us)
Async XLA Ops:
  1.5 0.9 copy-start.4
  69.2 1.3 %copy-start = (f32[2,16,32,512]{3,2,1,0:T(8,128)}, f32[2,16,32,512]{3,2,1,0:T(8,128)S(1)}, u32[]{:S(2)}) copy-start(f32[2,16,32,512]{3,2,1,0:T(8,128)S(1)} %get-tuple-element.14.rows_ref) | copy-start | bytes 6291460
  70.6 19.3 %copy-start.1 = (f32[2,16,32,512]{3,2,1,0:T(8,128)}, f32[2,16,32,512]{3,2,1,0:T(8,128)S(1)}, u32[]{:S(2)}) copy-start(f32[2,16,32,512]{3,2,1,0:T(8,128)S(1)} %get-tuple-element.15.cols_ref) | copy-start | bytes 6291460
  89.9 1.0 copy-start.2
  90.9 1.0 copy-start.3
where the time goes:
time: 106 us; the launch traced here: 105 us
  Pallas kernels  99.4 us (94%)
  local copies, waits for them, and re-layouts  5.1 us (5%)
    pallas_call x1, Pallas kernels, exchange(): pl.pallas_call(exchange_kernel, out_shape=(shape((m, n // 2 + 1, SUB, BLO...  66.8 us
    pallas_call x1, Pallas kernels, factorize(): pl.pallas_call(cholesky_kernel, out_shape=(shape, shape), in_specs=[vmem]...  19.3 us
    pallas_call x1, Pallas kernels, update(): pl.pallas_call(update_kernel, out_shape=(shape(flat.shape, jnp.float32),...  13.3 us
    unnamed x11, local copies, waits for them, and re-layouts  5.01 us

commit v1 on v0

--- a/solution.py
+++ b/solution.py
@@ -92,25 +92,6 @@
             extra[end:, :end] = extra[end:, :end] - dot_f32(turned, v_ref[here, :end], 1, 0)
 
 
-def factorize(a, width):
-    shape = jax.ShapeDtypeStruct((width, width), jnp.float32)
-    vmem = pl.BlockSpec(memory_space=pltpu.VMEM)
-    return pl.pallas_call(
-        cholesky_kernel,
-        out_shape=(shape, shape),
-        in_specs=[vmem],
-        out_specs=(vmem, vmem),
-        scratch_shapes=[
-            pltpu.VMEM((width, width), jnp.float32),
-            pltpu.VMEM((width, width), jnp.float32),
-            pltpu.VMEM((BLOCK, 2 * BLOCK), jnp.float32),
-        ],
-        compiler_params=pltpu.CompilerParams(vmem_limit_bytes=32 << 20),
-        cost_estimate=pl.CostEstimate(flops=1 << 32, bytes_accessed=4 << 20, transcendentals=0),
-        name="factorize",
-    )(a)
-
-
 def split(x):
     high = x.astype(jnp.bfloat16)
     return high, (x - high.astype(jnp.float32)).astype(jnp.bfloat16)
@@ -239,7 +220,7 @@
     tiles, pieces, side, width = rows.shape
     vmem = pl.BlockSpec(memory_space=pltpu.VMEM)
     smem = pl.BlockSpec(memory_space=pltpu.SMEM)
-    hbm = pl.BlockSpec(memory_space=pl.ANY)
+    hbm = pl.BlockSpec(memory_space=pltpu.HBM)
     flat = trailing.reshape(trailing.size // BLOCK, BLOCK)
     shape = jax.ShapeDtypeStruct
     return pl.pallas_call(
@@ -262,13 +243,13 @@
             pltpu.VMEM((width, side), jnp.float32),
             pltpu.SemaphoreType.DMA((2 * tiles,)),
         ],
-        compiler_params=pltpu.CompilerParams(vmem_limit_bytes=56 << 20),
+        compiler_params=pltpu.CompilerParams(vmem_limit_bytes=45 << 20),
         name="update",
     )(kept, near, scale, upper, inverse, rows, cols, flat)
 
 
-def exchange_kernel(
-    pack, own, gathered, rows, cols, first, turned,
+def panel_kernel(
+    pack, own, upper, inverse, rows, cols, gathered, first, turned, trail, extra, work,
     local_sems, turn_sems, send1, recv1, send2, recv2, send3, recv3, send4, recv4,
 ):
     p, q = lax.axis_index("prow"), lax.axis_index("pcol")
@@ -366,6 +347,8 @@
         return remote(own, rows.at[:, sender], send3.at[b], recv3.at[sender], p, b)
 
     others(q, m, lambda b: third_copy(b, q).start())
+
+    cholesky_kernel(gathered, upper, inverse, trail, extra, work)
 
     held.wait()
     others(p, n, lambda a: fourth_copy(a, a, core).wait_recv())
@@ -380,24 +363,29 @@
     others(p, n, lambda a: fourth_copy(a, p, lax.rem(a, 2)).wait_send())
 
 
-def exchange(pack, own):
+def panel_step(pack, own):
     n, m = lax.axis_size("prow"), lax.axis_size("pcol")
     tiles, side, width = own.shape
     vmem = pl.BlockSpec(memory_space=pltpu.VMEM)
     shape = jax.ShapeDtypeStruct
     dma = pltpu.SemaphoreType.DMA
     return pl.pallas_call(
-        exchange_kernel,
+        panel_kernel,
         out_shape=(
-            shape((m, n // 2 + 1, SUB, BLOCK), jnp.float32),
+            shape((width, width), jnp.float32),
+            shape((width, width), jnp.float32),
             shape((tiles, m, side, width), jnp.float32),
             shape((tiles, n, side, width), jnp.float32),
         ),
         in_specs=[vmem, vmem],
-        out_specs=(vmem, vmem, vmem),
+        out_specs=(vmem, vmem, vmem, vmem),
         scratch_shapes=[
+            pltpu.VMEM((m, n // 2 + 1, SUB, BLOCK), jnp.float32),
             pltpu.VMEM((n, SUB, BLOCK), jnp.float32),
             pltpu.VMEM((tiles, side, width), jnp.float32),
+            pltpu.VMEM((width, width), jnp.float32),
+            pltpu.VMEM((width, width), jnp.float32),
+            pltpu.VMEM((BLOCK, 2 * BLOCK), jnp.float32),
             dma((5,)), dma((4,)),
             dma((n,)), dma((n,)), dma((m,)), dma((m,)),
             dma((m,)), dma((m,)), dma((n,)), dma((n,)),
@@ -405,7 +393,7 @@
         compiler_params=pltpu.CompilerParams(
             collective_id=0, has_side_effects=True, vmem_limit_bytes=32 << 20
         ),
-        name="exchange",
+        name="panel",
     )(pack, own)
 
 
@@ -413,8 +401,7 @@
     side = diag_tile.shape[0]
     own = jnp.transpose(panel[:, 0], (0, 2, 1))
     pack = diag_tile.T.reshape(side // SUB, SUB, side).transpose(1, 0, 2).reshape(SUB, BLOCK)
-    gathered, rows, cols = exchange(pack, own)
-    upper, inverse = factorize(gathered, panel.shape[2])
+    upper, inverse, rows, cols = panel_step(pack, own)
     updated, factor, diag_out = update(
         kept, precision, tile_scale, upper, inverse, rows, cols, trailing
     )

time: 106 us -> 85 us (0.80)
  Pallas kernels: 99.4 us -> 79.3 us
  local copies, waits for them, and re-layouts: 5.1 us -> 3.96 us
    pallas_call x2 -> x1, Pallas kernels: 86.1 us -> 67 us  [panel_step(): pl.pallas_call(panel_kernel, out_shape=(shape((width, width), jnp.float32...]
    unnamed x11 -> x9, local copies, waits for them, and re-layouts: 5.01 us -> 3.87 us
where the time goes in v1:
time: 85 us; the launch traced here: 84.1 us
  Pallas kernels  79.3 us (93%)
  local copies, waits for them, and re-layouts  3.96 us (5%)
    pallas_call x1, Pallas kernels, panel_step(): pl.pallas_call(panel_kernel, out_shape=(shape((width, width), jnp.float32...  67 us
    pallas_call x1, Pallas kernels, update(): pl.pallas_call(update_kernel, out_shape=(shape(flat.shape, jnp.float32),...  12.4 us
    unnamed x9, local copies, waits for them, and re-layouts  3.87 us

profile of v1, /device:TPU:176, one launch (start us, length us, event | category | flops | bytes accessed | tf_op | source)
XLA Modules:
  0.0 84.1 jit_solution(6669321926354686044)
XLA Ops:
  0.6 0.8 copy.12
  1.4 0.1 reshape.19.pack
  1.5 0.0 copy-start
  1.5 0.9 %copy-done = f32[2,1,512,32]{2,3,1,0:T(8,128)S(1)} copy-done((f32[2,1,512,32]{2,3,1,0:T(8,128)S(1)}, f32[2,1,512,32]{2,3,1,0:T(8,128)}, u32[]{:S(2)}) %copy-start) | copy-done | bytes 131096
  2.4 67.0 %panel.1 = (f32[512,512]{1,0:T(8,128)S(1)}, f32[512,512]{1,0:T(8,128)S(1)}, f32[2,16,32,512]{3,2,1,0:T(8,128)S(1)}, f32[2,16,32,512]{3,2,1,0:T(8,128)S(1)}) custom-call(f32[8,128]{1,0:T(8,128)S(1)} %reshape.19.pack, f32[2,32,512]{2,1,0:T(8,128)S(1)} %bitcast.15), custom_call_target="tpu_custom_call" | custom-call | tf_op jit(solution)/shard_map/panel/pallas_call | solution.py:372
  69.4 0.0 copy-start.1
  69.4 0.7 copy-done.1
  70.1 0.0 copy-start.2
  70.1 0.7 copy-done.2
  70.8 0.0 copy-start.3
  70.8 0.7 copy-done.3
  71.6 12.4 %update.1 = (f32[8192,128]{1,0:T(8,128)}, f32[2,32,512]{2,1,0:T(8,128)}, f32[32,32]{1,0:T(8,128)}) custom-call(s32[33,33]{1,0:T(8,128)S(1)} %copy-done.1, s32[33,33]{1,0:T(8,128)S(1)} %copy-done.2, f32[33,33]{1,0:T(8,128)S(1)} %copy-done.3, f32[512,512]{1,0:T(8,128)S(1)} %get-tuple-element.10.u_ref, f32[512,512]{1,0:T(8,128)S(1)} %get-tuple-element.11.v_ref, ...), custom_call_target="tpu_custom_call" | custom-call | tf_op jit(solution)/shard_map/update/pallas_call | solution.py:226
  (1 shorter events, 0.0 us)
Async XLA Ops:
  1.5 0.9 %copy-start = (f32[2,1,512,32]{2,3,1,0:T(8,128)S(1)}, f32[2,1,512,32]{2,3,1,0:T(8,128)}, u32[]{:S(2)}) copy-start(f32[2,1,512,32]{2,3,1,0:T(8,128)} %param.7) | copy-start | bytes 393220
  69.4 0.7 copy-start.1
  70.1 0.7 copy-start.2
  70.8 0.7 copy-start.3

commit v2 on v1

--- a/solution.py
+++ b/solution.py
@@ -8,6 +8,7 @@
 BLOCK = 128
 PANEL = 16
 SUB = 8
+ACROSS = 4
 FULL = lax.Precision.HIGHEST
 
 
@@ -60,7 +61,7 @@
             work[rest:, :] = work[rest:, :] - change
 
 
-def cholesky_kernel(gathered, u_ref, v_ref, trail, extra, work):
+def cholesky_kernel(gathered, u_ref, v_ref, trail, extra, work, between):
     width = u_ref.shape[0]
     assemble(gathered, trail, extra)
     u_ref[...] = jnp.zeros_like(u_ref)
@@ -75,6 +76,8 @@
         work[:, :BLOCK] = trail[here, here]
         work[:, BLOCK:] = eye
         factor_block(work)
+        if base == 0:
+            between()
         inverse = work[:, BLOCK:]
         u_ref[here, here] = jnp.where(row <= col, work[:, :BLOCK], 0.0)
         v_ref[here, here] = inverse
@@ -133,7 +136,7 @@
     kept, near, scale, u_ref, v_ref, rows_ref, cols_ref, trailing, out_hbm, factor_ref, diag_ref,
     current, result, srow, frow_h, frow_l, scol_h, scol_l, turned, sems,
 ):
-    tiles, pieces, side, width = rows_ref.shape
+    tiles, pieces, side, width = cols_ref.shape
     p, q = lax.axis_index("prow"), lax.axis_index("pcol")
     rows_all = lax.axis_size("prow")
     cols_all = lax.axis_size("pcol")
@@ -217,7 +220,7 @@
 
 
 def update(kept, near, scale, upper, inverse, rows, cols, trailing):
-    tiles, pieces, side, width = rows.shape
+    tiles, pieces, side, width = cols.shape
     vmem = pl.BlockSpec(memory_space=pltpu.VMEM)
     smem = pl.BlockSpec(memory_space=pltpu.SMEM)
     hbm = pl.BlockSpec(memory_space=pltpu.HBM)
@@ -254,7 +257,7 @@
 ):
     p, q = lax.axis_index("prow"), lax.axis_index("pcol")
     n, m = lax.axis_size("prow"), lax.axis_size("pcol")
-    keep = gathered.shape[1]
+    keep, across = gathered.shape[1], rows.shape[2]
     mesh_id = pl.DeviceIdType.MESH
 
     def others(me, count, body):
@@ -340,26 +343,60 @@
     block.wait()
     others(q, m, lambda b: second_copy(b, b).wait_recv())
 
-    whole = pltpu.make_async_copy(own, rows.at[:, q], local_sems.at[4])
-    whole.start()
-
-    def third_copy(b, sender):
-        return remote(own, rows.at[:, sender], send3.at[b], recv3.at[sender], p, b)
-
-    others(q, m, lambda b: third_copy(b, q).start())
-
-    cholesky_kernel(gathered, upper, inverse, trail, extra, work)
+    y, x = q // across, lax.rem(q, across)
+    whole = [
+        pltpu.make_async_copy(own.at[t], rows.at[t, y, x], local_sems.at[4 + t])
+        for t in range(2)
+    ]
+    for copy in whole:
+        copy.start()
+
+    def near_x(to, sender):
+        return remote(
+            own.at[0], rows.at[0, y, sender], send3.at[0, to], recv3.at[0, sender],
+            p, y * across + to,
+        )
+
+    def near_y(to, sender):
+        return remote(
+            own.at[1], rows.at[1, sender, x], send3.at[1, to], recv3.at[1, sender],
+            p, to * across + x,
+        )
+
+    def far_y(to, sender):
+        part = rows.at[0, sender]
+        return remote(part, part, send3.at[2, to], recv3.at[2, sender], p, to * across + x)
+
+    def far_x(to, sender):
+        part = rows.at[1, :, sender]
+        return remote(part, part, send3.at[3, to], recv3.at[3, sender], p, y * across + to)
+
+    others(x, across, lambda b: near_x(b, x).start())
+    others(y, across, lambda b: near_y(b, y).start())
+
+    def between():
+        for copy in whole:
+            copy.wait()
+        others(x, across, lambda b: near_x(b, b).wait_recv())
+        others(y, across, lambda b: near_y(b, b).wait_recv())
+        others(y, across, lambda b: far_y(b, y).start())
+        others(x, across, lambda b: far_x(b, x).start())
+
+    cholesky_kernel(gathered, upper, inverse, trail, extra, work, between)
 
     held.wait()
     others(p, n, lambda a: fourth_copy(a, a, core).wait_recv())
     partner = remote(cols.at[core], cols.at[core], turn_sems.at[2], turn_sems.at[3], other, q)
     partner.start()
-    whole.wait()
-    others(q, m, lambda b: third_copy(b, b).wait_recv())
+    others(y, across, lambda b: far_y(b, b).wait_recv())
+    others(x, across, lambda b: far_x(b, b).wait_recv())
     partner.wait()
     others(p, n, lambda a: first_copy(a, p).wait_send())
     others(q, m, lambda b: second_copy(b, q).wait_send())
-    others(q, m, lambda b: third_copy(b, q).wait_send())
+    others(x, across, lambda b: near_x(b, x).wait_send())
+    others(y, across, lambda b: near_y(b, y).wait_send())
+    others(y, across, lambda b: far_y(b, y).wait_send())
+    others(x, across, lambda b: far_x(b, x).wait_send())
     others(p, n, lambda a: fourth_copy(a, p, lax.rem(a, 2)).wait_send())
 
 
@@ -374,7 +411,7 @@
         out_shape=(
             shape((width, width), jnp.float32),
             shape((width, width), jnp.float32),
-            shape((tiles, m, side, width), jnp.float32),
+            shape((tiles, m // ACROSS, ACROSS, side, width), jnp.float32),
             shape((tiles, n, side, width), jnp.float32),
         ),
         in_specs=[vmem, vmem],
@@ -386,12 +423,15 @@
             pltpu.VMEM((width, width), jnp.float32),
             pltpu.VMEM((width, width), jnp.float32),
             pltpu.VMEM((BLOCK, 2 * BLOCK), jnp.float32),
-            dma((5,)), dma((4,)),
+            dma((6,)), dma((4,)),
             dma((n,)), dma((n,)), dma((m,)), dma((m,)),
-            dma((m,)), dma((m,)), dma((n,)), dma((n,)),
+            dma((4, ACROSS)), dma((4, ACROSS)), dma((n,)), dma((n,)),
         ],
         compiler_params=pltpu.CompilerParams(
             collective_id=0, has_side_effects=True, vmem_limit_bytes=32 << 20
+        ),
+        cost_estimate=pl.CostEstimate(
+            flops=1 << 34, bytes_accessed=1 << 26, transcendentals=0
         ),
         name="panel",
     )(pack, own)

time: 85 us -> 75.7 us (0.89)
  the two profiles are of different devices: /device:TPU:176 before, /device:TPU:41 now
where the time goes in v2:
time: 75.7 us; the launch traced here: 75.6 us
  Pallas kernels  72.9 us (96%)
  local copies, waits for them, and re-layouts  1.8 us (2%)
  between operations  0.83 us (1%)
    pallas_call x1, Pallas kernels, panel_step(): pl.pallas_call(panel_kernel, out_shape=(shape((width, width), jnp.float32...  59.7 us
    pallas_call x1, Pallas kernels, update(): pl.pallas_call(update_kernel, out_shape=(shape(flat.shape, jnp.float32),...  13.3 us
    unnamed x9, local copies, waits for them, and re-layouts  1.71 us

profile of v2, /device:TPU:41, one launch (start us, length us, event | category | flops | bytes accessed | tf_op | source)
XLA Modules:
  0.0 75.6 jit_solution(11665105287146121673)
XLA Ops:
  0.6 0.8 %copy.12 = f32[32,32]{0,1:T(8,128)S(1)} copy(f32[32,32]{1,0:T(8,128)} %param.6) | data formatting | bytes 8192 | tf_op args[0]
  1.4 0.1 reshape.19.pack
  1.5 0.0 copy-start.3
  1.5 0.9 %copy-done.3 = f32[2,1,512,32]{2,3,1,0:T(8,128)S(1)} copy-done((f32[2,1,512,32]{2,3,1,0:T(8,128)S(1)}, f32[2,1,512,32]{2,3,1,0:T(8,128)}, u32[]{:S(2)}) %copy-start.3) | copy-done | bytes 131096
  2.4 0.0 copy-start
  2.4 0.0 copy-start.1
  2.4 0.0 copy-start.2
  2.4 59.7 %panel.1 = (f32[512,512]{1,0:T(8,128)S(1)}, f32[512,512]{1,0:T(8,128)S(1)}, f32[2,4,4,32,512]{4,3,2,1,0:T(8,128)S(1)}, f32[2,16,32,512]{3,2,1,0:T(8,128)S(1)}) custom-call(f32[8,128]{1,0:T(8,128)S(1)} %reshape.19.pack, f32[2,32,512]{2,1,0:T(8,128)S(1)} %bitcast.15), custom_call_target="tpu_custom_call" | custom-call | flops 17179869184 | bytes 67108864 | tf_op jit(solution)/shard_map/panel/pallas_call | solution.py:409
  62.1 0.0 copy-done
  62.1 0.0 copy-done.1
  62.1 0.0 copy-done.2
  62.1 13.3 %update.1 = (f32[8192,128]{1,0:T(8,128)}, f32[2,32,512]{2,1,0:T(8,128)}, f32[32,32]{1,0:T(8,128)}) custom-call(s32[33,33]{1,0:T(8,128)S(1)} %copy-done, s32[33,33]{1,0:T(8,128)S(1)} %copy-done.1, f32[33,33]{1,0:T(8,128)S(1)} %copy-done.2, f32[512,512]{1,0:T(8,128)S(1)} %get-tuple-element.10.u_ref, f32[512,512]{1,0:T(8,128)S(1)} %get-tuple-element.11.v_ref, ...), custom_call_target="tpu_custom_call" | custom-call | tf_op jit(solution)/shard_map/update/pallas_call | solution.py:229
  (1 shorter events, 0.0 us)
Async XLA Ops:
  1.5 0.9 %copy-start.3 = (f32[2,1,512,32]{2,3,1,0:T(8,128)S(1)}, f32[2,1,512,32]{2,3,1,0:T(8,128)}, u32[]{:S(2)}) copy-start(f32[2,1,512,32]{2,3,1,0:T(8,128)} %param.7) | copy-start | bytes 393220
  2.4 59.7 %copy-start = (s32[33,33]{1,0:T(8,128)S(1)}, s32[33,33]{1,0:T(8,128)}, u32[]{:S(2)}) copy-start(s32[33,33]{1,0:T(8,128)} %kept.1) | copy-start | bytes 13072
  2.4 59.7 %copy-start.1 = (s32[33,33]{1,0:T(8,128)S(1)}, s32[33,33]{1,0:T(8,128)}, u32[]{:S(2)}) copy-start(s32[33,33]{1,0:T(8,128)} %near.1) | copy-start | bytes 13072
  2.4 59.7 %copy-start.2 = (f32[33,33]{1,0:T(8,128)S(1)}, f32[33,33]{1,0:T(8,128)}, u32[]{:S(2)}) copy-start(f32[33,33]{1,0:T(8,128)} %scale.1) | copy-start | bytes 13072

commit v3 on v2

--- a/solution.py
+++ b/solution.py
@@ -133,10 +133,10 @@
 
 
 def update_kernel(
-    kept, near, scale, u_ref, v_ref, rows_ref, cols_ref, trailing, out_hbm, factor_ref, diag_ref,
-    current, result, srow, frow_h, frow_l, scol_h, scol_l, turned, sems,
+    kept, near, scale, u_ref, rows_ref, cols_ref, trailing, out_hbm, factor_ref, diag_ref,
+    current, result, frow_h, frow_l, scol_h, scol_l, turned, sems,
 ):
-    tiles, pieces, side, width = cols_ref.shape
+    tiles, side, width = factor_ref.shape
     p, q = lax.axis_index("prow"), lax.axis_index("pcol")
     rows_all = lax.axis_size("prow")
     cols_all = lax.axis_size("pcol")
@@ -152,27 +152,18 @@
         load.start()
     turned[...] = u_ref[pl.ds(pl.multiple_of(q * side, side), side), :].T
     diag_ref[...] = turned[pl.ds(pl.multiple_of(p * side, side), side), :]
-    mid = width // 2
-
-    def solve(piece):
-        top = dot_f32(v_ref[:mid, :mid], piece[:mid, :], 1, 0)
-        low = dot_f32(v_ref[mid:, :], piece, 1, 0)
-        return jnp.concatenate([top, low], 0)
-
     for r in range(tiles):
         keep = kept[r * rows_all + p + 1, 0].astype(jnp.float32)
-        solved = solve(rows_ref[r].reshape(width, width)) * keep
-        srow[r] = solved
+        solved = rows_ref[r] * keep
+        factor_ref[r] = rows_ref[r, pl.ds(pl.multiple_of(q * side, side), side), :] * keep
         high, low = split(solved.T)
         frow_h[r] = high
         frow_l[r] = low
     for t in range(tiles):
         keep = kept[t * cols_all + q + 1, 0].astype(jnp.float32)
-        high, low = split(solve(cols_ref[t].reshape(width, width)) * keep)
+        high, low = split(cols_ref[t] * keep)
         scol_h[t] = high
         scol_l[t] = low
-    for r in range(tiles):
-        factor_ref[r] = srow[r, pl.ds(pl.multiple_of(q * side, side), side), :]
 
     def dot_half(a, b):
         return jnp.dot(a, b, preferred_element_type=jnp.float32)
@@ -219,8 +210,8 @@
         store.wait()
 
 
-def update(kept, near, scale, upper, inverse, rows, cols, trailing):
-    tiles, pieces, side, width = cols.shape
+def update(kept, near, scale, upper, rows, cols, side, trailing):
+    tiles, width = cols.shape[:2]
     vmem = pl.BlockSpec(memory_space=pltpu.VMEM)
     smem = pl.BlockSpec(memory_space=pltpu.SMEM)
     hbm = pl.BlockSpec(memory_space=pltpu.HBM)
@@ -233,12 +224,11 @@
             shape((tiles, side, width), jnp.float32),
             shape((side, side), jnp.float32),
         ),
-        in_specs=[smem, smem, smem, vmem, vmem, vmem, vmem, hbm],
+        in_specs=[smem, smem, smem, vmem, vmem, vmem, hbm],
         out_specs=(hbm, vmem, vmem),
         scratch_shapes=[
             pltpu.VMEM(flat.shape, jnp.float32),
             pltpu.VMEM(flat.shape, jnp.float32),
-            pltpu.VMEM((tiles, width, width), jnp.float32),
             pltpu.VMEM((tiles, width, width), jnp.bfloat16),
             pltpu.VMEM((tiles, width, width), jnp.bfloat16),
             pltpu.VMEM((tiles, width, width), jnp.bfloat16),
@@ -248,16 +238,17 @@
         ],
         compiler_params=pltpu.CompilerParams(vmem_limit_bytes=45 << 20),
         name="update",
-    )(kept, near, scale, upper, inverse, rows, cols, flat)
+    )(kept, near, scale, upper, rows, cols, flat)
 
 
 def panel_kernel(
-    pack, own, upper, inverse, rows, cols, gathered, first, turned, trail, extra, work,
+    pack, own, upper, row_solved, col_solved,
+    inverse, rows, cols, gathered, first, turned, trail, extra, work,
     local_sems, turn_sems, send1, recv1, send2, recv2, send3, recv3, send4, recv4,
 ):
     p, q = lax.axis_index("prow"), lax.axis_index("pcol")
     n, m = lax.axis_size("prow"), lax.axis_size("pcol")
-    keep, across = gathered.shape[1], rows.shape[2]
+    keep, across, width = gathered.shape[1], rows.shape[2], upper.shape[0]
     mesh_id = pl.DeviceIdType.MESH
 
     def others(me, count, body):
@@ -287,6 +278,9 @@
             device_id=(a, b), device_id_type=mesh_id,
         )
 
+    core = lax.rem(p, 2)
+    other = p + 1 - 2 * core
+
     slot = lax.rem(p + m - q, m)
     mine = pltpu.make_async_copy(pack, first.at[slot], local_sems.at[0])
     mine.start()
@@ -311,37 +305,22 @@
     mine.wait()
     others(p, n, lambda a: first_copy(a, a).wait_recv())
 
-    part = first.at[pl.ds(0, keep)]
-    block = pltpu.make_async_copy(part, gathered.at[q], local_sems.at[2])
+    share = pl.ds(core * (keep // 2), keep // 2)
+    part = first.at[share]
+    block = pltpu.make_async_copy(part, gathered.at[q, share], local_sems.at[2])
     block.start()
 
     def second_copy(b, sender):
-        return remote(part, gathered.at[sender], send2.at[b], recv2.at[sender], p, b)
+        return remote(part, gathered.at[sender, share], send2.at[b], recv2.at[sender], p, b)
 
     others(q, m, lambda b: second_copy(b, q).start())
-
-    @pl.when(p != q)
-    def _():
-        swap.wait()
-
-    @pl.when(p == q)
-    def _():
-        stay.wait()
-
-    core = lax.rem(p, 2)
-    other = p + 1 - 2 * core
-    held = pltpu.make_async_copy(turned.at[core], cols.at[core, p], local_sems.at[3])
-    held.start()
-
-    def fourth_copy(a, sender, tile):
-        return remote(
-            turned.at[tile], cols.at[tile, sender], send4.at[a], recv4.at[sender], a, q
-        )
-
-    others(p, n, lambda a: fourth_copy(a, p, lax.rem(a, 2)).start())
 
     block.wait()
     others(q, m, lambda b: second_copy(b, b).wait_recv())
+    fill = remote(
+        gathered.at[:, share], gathered.at[:, share], turn_sems.at[4], turn_sems.at[5], other, q
+    )
+    fill.start()
 
     y, x = q // across, lax.rem(q, across)
     whole = [
@@ -374,6 +353,24 @@
     others(x, across, lambda b: near_x(b, x).start())
     others(y, across, lambda b: near_y(b, y).start())
 
+    @pl.when(p != q)
+    def _():
+        swap.wait()
+
+    @pl.when(p == q)
+    def _():
+        stay.wait()
+
+    held = pltpu.make_async_copy(turned.at[core], cols.at[core, p], local_sems.at[3])
+    held.start()
+
+    def fourth_copy(a, sender, tile):
+        return remote(
+            turned.at[tile], cols.at[tile, sender], send4.at[a], recv4.at[sender], a, q
+        )
+
+    others(p, n, lambda a: fourth_copy(a, p, lax.rem(a, 2)).start())
+
     def between():
         for copy in whole:
             copy.wait()
@@ -382,15 +379,26 @@
         others(y, across, lambda b: far_y(b, y).start())
         others(x, across, lambda b: far_x(b, x).start())
 
+    fill.wait()
     cholesky_kernel(gathered, upper, inverse, trail, extra, work, between)
 
+    def solve(piece):
+        mid = width // 2
+        top = dot_f32(inverse[:mid, :mid], piece[:mid, :], 1, 0)
+        low = dot_f32(inverse[mid:, :], piece, 1, 0)
+        return jnp.concatenate([top, low], 0)
+
+    others(y, across, lambda b: far_y(b, b).wait_recv())
+    others(x, across, lambda b: far_x(b, b).wait_recv())
+    row_solved[0] = solve(rows[0].reshape(width, width))
     held.wait()
     others(p, n, lambda a: fourth_copy(a, a, core).wait_recv())
     partner = remote(cols.at[core], cols.at[core], turn_sems.at[2], turn_sems.at[3], other, q)
     partner.start()
-    others(y, across, lambda b: far_y(b, b).wait_recv())
-    others(x, across, lambda b: far_x(b, b).wait_recv())
+    row_solved[1] = solve(rows[1].reshape(width, width))
+    col_solved[core] = solve(cols[core].reshape(width, width))
     partner.wait()
+    col_solved[1 - core] = solve(cols[1 - core].reshape(width, width))
     others(p, n, lambda a: first_copy(a, p).wait_send())
     others(q, m, lambda b: second_copy(b, q).wait_send())
     others(x, across, lambda b: near_x(b, x).wait_send())
@@ -410,20 +418,22 @@
         panel_kernel,
         out_shape=(
             shape((width, width), jnp.float32),
-            shape((width, width), jnp.float32),
-            shape((tiles, m // ACROSS, ACROSS, side, width), jnp.float32),
-            shape((tiles, n, side, width), jnp.float32),
+            shape((tiles, width, width), jnp.float32),
+            shape((tiles, width, width), jnp.float32),
         ),
         in_specs=[vmem, vmem],
-        out_specs=(vmem, vmem, vmem, vmem),
+        out_specs=(vmem, vmem, vmem),
         scratch_shapes=[
-            pltpu.VMEM((m, n // 2 + 1, SUB, BLOCK), jnp.float32),
+            pltpu.VMEM((width, width), jnp.float32),
+            pltpu.VMEM((tiles, m // ACROSS, ACROSS, side, width), jnp.float32),
+            pltpu.VMEM((tiles, n, side, width), jnp.float32),
+            pltpu.VMEM((m, n // 2 + 2, SUB, BLOCK), jnp.float32),
             pltpu.VMEM((n, SUB, BLOCK), jnp.float32),
             pltpu.VMEM((tiles, side, width), jnp.float32),
             pltpu.VMEM((width, width), jnp.float32),
             pltpu.VMEM((width, width), jnp.float32),
             pltpu.VMEM((BLOCK, 2 * BLOCK), jnp.float32),
-            dma((6,)), dma((4,)),
+            dma((6,)), dma((6,)),
             dma((n,)), dma((n,)), dma((m,)), dma((m,)),
             dma((4, ACROSS)), dma((4, ACROSS)), dma((n,)), dma((n,)),
         ],
@@ -441,9 +451,9 @@
     side = diag_tile.shape[0]
     own = jnp.transpose(panel[:, 0], (0, 2, 1))
     pack = diag_tile.T.reshape(side // SUB, SUB, side).transpose(1, 0, 2).reshape(SUB, BLOCK)
-    upper, inverse, rows, cols = panel_step(pack, own)
+    upper, rows, cols = panel_step(pack, own)
     updated, factor, diag_out = update(
-        kept, precision, tile_scale, upper, inverse, rows, cols, trailing
+        kept, precision, tile_scale, upper, rows, cols, side, trailing
     )
     factor_out = jnp.transpose(factor, (0, 2, 1))[:, None]
     return (diag_out, factor_out, updated.reshape(trailing.shape))

time: 75.7 us -> 73.7 us (0.974)
  the two profiles are of different devices: /device:TPU:41 before, /device:TPU:5 now
where the time goes in v3:
time: 73.7 us; the launch traced here: 73.8 us
  Pallas kernels  71.2 us (97%)
  local copies, waits for them, and re-layouts  1.8 us (2%)
  between operations  0.83 us (1%)
    pallas_call x1, Pallas kernels, panel_step(): pl.pallas_call(panel_kernel, out_shape=(shape((width, width), jnp.float32...  62.7 us
    pallas_call x1, Pallas kernels, update(): pl.pallas_call(update_kernel, out_shape=(shape(flat.shape, jnp.float32),...  8.45 us
    unnamed x9, local copies, waits for them, and re-layouts  1.71 us

profile of v3, /device:TPU:5, one launch (start us, length us, event | category | flops | bytes accessed | tf_op | source)
XLA Modules:
  0.0 73.8 jit_solution(2478335145557360483)
XLA Ops:
  0.6 0.8 %copy.12 = f32[32,32]{0,1:T(8,128)S(1)} copy(f32[32,32]{1,0:T(8,128)} %param.6) | data formatting | bytes 8192 | tf_op args[0]
  1.4 0.1 reshape.19.pack
  1.5 0.0 copy-start.3
  1.5 0.9 %copy-done.3 = f32[2,1,512,32]{2,3,1,0:T(8,128)S(1)} copy-done((f32[2,1,512,32]{2,3,1,0:T(8,128)S(1)}, f32[2,1,512,32]{2,3,1,0:T(8,128)}, u32[]{:S(2)}) %copy-start.3) | copy-done | bytes 131096
  2.4 0.0 copy-start
  2.4 0.0 copy-start.1
  2.4 0.0 copy-start.2
  2.4 62.7 %panel.1 = (f32[512,512]{1,0:T(8,128)S(1)}, f32[2,512,512]{2,1,0:T(8,128)S(1)}, f32[2,512,512]{2,1,0:T(8,128)S(1)}) custom-call(f32[8,128]{1,0:T(8,128)S(1)} %reshape.19.pack, f32[2,32,512]{2,1,0:T(8,128)S(1)} %bitcast.15), custom_call_target="tpu_custom_call" | custom-call | flops 17179869184 | bytes 67108864 | tf_op jit(solution)/shard_map/panel/pallas_call | solution.py:417
  65.2 0.0 copy-done
  65.2 0.0 copy-done.1
  65.2 0.0 copy-done.2
  65.2 8.4 %update.1 = (f32[8192,128]{1,0:T(8,128)}, f32[2,32,512]{2,1,0:T(8,128)}, f32[32,32]{1,0:T(8,128)}) custom-call(s32[33,33]{1,0:T(8,128)S(1)} %copy-done, s32[33,33]{1,0:T(8,128)S(1)} %copy-done.1, f32[33,33]{1,0:T(8,128)S(1)} %copy-done.2, f32[512,512]{1,0:T(8,128)S(1)} %get-tuple-element.9.u_ref, f32[2,512,512]{2,1,0:T(8,128)S(1)} %get-tuple-element.10.rows_ref, ...), custom_call_target="tpu_custom_call" | custom-call | tf_op jit(solution)/shard_map/update/pallas_call | solution.py:220
  (1 shorter events, 0.0 us)
Async XLA Ops:
  1.5 0.9 %copy-start.3 = (f32[2,1,512,32]{2,3,1,0:T(8,128)S(1)}, f32[2,1,512,32]{2,3,1,0:T(8,128)}, u32[]{:S(2)}) copy-start(f32[2,1,512,32]{2,3,1,0:T(8,128)} %param.7) | copy-start | bytes 393220
  2.4 62.7 %copy-start = (s32[33,33]{1,0:T(8,128)S(1)}, s32[33,33]{1,0:T(8,128)}, u32[]{:S(2)}) copy-start(s32[33,33]{1,0:T(8,128)} %kept.1) | copy-start | bytes 13072
  2.4 62.8 %copy-start.1 = (s32[33,33]{1,0:T(8,128)S(1)}, s32[33,33]{1,0:T(8,128)}, u32[]{:S(2)}) copy-start(s32[33,33]{1,0:T(8,128)} %near.1) | copy-start | bytes 13072
  2.4 62.8 %copy-start.2 = (f32[33,33]{1,0:T(8,128)S(1)}, f32[33,33]{1,0:T(8,128)}, u32[]{:S(2)}) copy-start(f32[33,33]{1,0:T(8,128)} %scale.1) | copy-start | bytes 13072
